TPU v7x, 1024 devices: a whole 4x8x16 slice. The times are simulated.
1024 devices in a mesh: side: 2 (over x_hi), grp: 32 (over x_lo, z), rep: 16 (over y, core).
Axes of the slice: x: 4 (x_hi: 2, x_lo: 2; x = x_hi * 2 + x_lo), y: 8, z: 16, core: 2. Of those that a mesh axis runs over, the one named last changes fastest.
Arguments:
- tokens: bfloat16 [2048, 4096], P('grp', ('side', 'rep')), may hold values from -6 to 6
- grad_out: bfloat16 [2048, 4096], P('grp', ('side', 'rep')), may hold values from -1.5 to 1.5
- route: int32 [2048, 2], P('grp'), may hold values from 0 to 31, all different within a row; in each aligned block of 64 rows (0 to 63, 64 to 127, ...) at most 8 rows name the same one
- gate: bfloat16 [2048, 2], P('grp'), may hold values from 0.099609375 to 1
- w_gate: bfloat16 [32, 4096, 4096], P('grp', None, ('side', 'rep')), may hold values from -0.09375 to 0.09375
- w_up: bfloat16 [32, 4096, 4096], P('grp', None, ('side', 'rep')), may hold values from -0.09375 to 0.09375
- w_down: bfloat16 [32, 4096, 4096], P('grp', ('side', 'rep')), may hold values from -0.09375 to 0.09375
Outputs:
- layer_out: bfloat16 [2048, 4096], P('grp', ('side', 'rep'))
- grad_tokens: bfloat16 [2048, 4096], P('grp', ('side', 'rep'))
- gate_grad: float32 [2048, 2], P('grp')
Inputs may be any that keep to these rules, and one draw needn't show every extreme that they name: `route`: each row names two different experts. Within each aligned block of 64 rows no expert is named by more than 8 rows, and in some block one expert is named by exactly 8 rows.
All inputs are finite; a program needn't handle non-finite values.
Results may differ from a plain program's by a relative error of at most 0.009.
Values may be sent and summed in bfloat16 or wider, within the bound.
No kernel may reach another device: no remote copies, remote signals or barrier semaphores. Data moves between devices by JAX's collectives and lax.ppermute only.
A program may use at most 32 MiB of HBM per device.

v0:
```python
import jax
import jax.numpy as jnp
from jax import lax
from jax.sharding import PartitionSpec as P

CAP = 8


def unit_math(pre_gate, pre_up, back, coef):
    sigma = jax.nn.sigmoid(pre_gate)
    active = pre_gate * sigma
    hidden = (active * pre_up).astype(jnp.bfloat16)
    partial_gate = jnp.sum(hidden.astype(jnp.float32) * back, axis=tuple(range(1, back.ndim)))
    d_hidden = coef * back
    d_gate = (d_hidden * pre_up * sigma * (1.0 + pre_gate * (1.0 - sigma))).astype(jnp.bfloat16)
    d_up = (d_hidden * active).astype(jnp.bfloat16)
    return (hidden, d_gate, d_up, partial_gate)


def local(tokens, grad_out, route, gate, w_gate, w_up, w_down):
    groups = lax.axis_size("grp")
    tok_rows = tokens.shape[0]
    flat = route.reshape(-1)
    count = flat.shape[0]
    onehot = (flat[:, None] == jnp.arange(groups, dtype=jnp.int32)[None, :]).astype(jnp.int32)
    earlier = jnp.cumsum(onehot, axis=0) - onehot
    target = flat * CAP + jnp.sum(earlier * onehot, axis=1)
    slots = groups * CAP
    places = (jnp.arange(slots, dtype=jnp.int32)[:, None] == target[None, :]).astype(jnp.float32)
    owner = jnp.arange(count, dtype=jnp.int32) // 2
    tok_map = (owner[:, None] == jnp.arange(tok_rows, dtype=jnp.int32)[None, :]).astype(jnp.float32)
    picks = jnp.dot(places, tok_map, precision=lax.Precision.HIGHEST)
    picks_low = picks.astype(jnp.bfloat16)
    send_x = (
        jnp.dot(picks_low, tokens, preferred_element_type=jnp.float32)
        .astype(jnp.bfloat16)
        .reshape(groups, CAP, -1)
    )
    send_dy = (
        jnp.dot(picks_low, grad_out, preferred_element_type=jnp.float32)
        .astype(jnp.bfloat16)
        .reshape(groups, CAP, -1)
    )
    send_gate = (
        jnp.dot(places.astype(jnp.bfloat16), gate.reshape(-1), preferred_element_type=jnp.float32)
        .astype(jnp.bfloat16)
        .reshape(groups, CAP)
    )
    recv_x, recv_dy, recv_gate = (
        lax.all_to_all(send_x, "grp", split_axis=0, concat_axis=0, tiled=True),
        lax.all_to_all(send_dy, "grp", split_axis=0, concat_axis=0, tiled=True),
        lax.all_to_all(send_gate, "grp", split_axis=0, concat_axis=0, tiled=True),
    )
    coef = recv_gate.reshape(-1).astype(jnp.float32)
    full_x, full_dy = (
        lax.all_gather(recv_x, ("side", "rep"), axis=2, tiled=True),
        lax.all_gather(recv_dy, ("side", "rep"), axis=2, tiled=True),
    )
    rows_x = full_x.reshape(slots, -1)
    rows_dy = full_dy.reshape(slots, -1)
    wg = w_gate[0]
    wu = w_up[0]
    wd = w_down[0]
    pre_gate = jnp.dot(rows_x, wg, preferred_element_type=jnp.float32)
    pre_up = jnp.dot(rows_x, wu, preferred_element_type=jnp.float32)
    back = lax.dot_general(
        rows_dy, wd, (((1,), (1,)), ((), ())), preferred_element_type=jnp.float32
    )
    hidden, d_gate, d_up, partial_gate = unit_math(pre_gate, pre_up, back, coef[:, None])
    gate_total = lax.psum(partial_gate, ("side", "rep"))
    input_term = lax.dot_general(
        wg, d_gate, (((1,), (1,)), ((), ())), preferred_element_type=jnp.float32
    )
    input_term = input_term + lax.dot_general(
        wu, d_up, (((1,), (1,)), ((), ())), preferred_element_type=jnp.float32
    )
    layer_term = lax.dot_general(
        wd, hidden, (((0,), (1,)), ((), ())), preferred_element_type=jnp.float32
    )
    local_out = lax.psum_scatter(
        jnp.concatenate([input_term, layer_term], axis=1),
        ("side", "rep"),
        scatter_dimension=0,
        tiled=True,
    )
    columns = local_out.shape[0]
    parts = local_out.reshape(columns, 2, groups, CAP)
    back_out, back_gate = (
        lax.all_to_all(parts, "grp", split_axis=2, concat_axis=2, tiled=True),
        lax.all_to_all(
            gate_total.reshape(1, 1, groups, CAP), "grp", split_axis=2, concat_axis=2, tiled=True
        ),
    )
    back_out = back_out.reshape(columns, 2, slots)
    weighted = tok_map * gate.reshape(-1).astype(jnp.float32)[:, None]
    combine = jnp.dot(places, weighted, precision=lax.Precision.HIGHEST)
    grad_cols = jnp.dot(back_out[:, 0, :], picks, precision=lax.Precision.HIGHEST)
    layer_cols = jnp.dot(back_out[:, 1, :], combine, precision=lax.Precision.HIGHEST)
    gate_grad = jnp.dot(back_gate.reshape(slots), places, precision=lax.Precision.HIGHEST).reshape(
        tok_rows, 2
    )
    return (layer_cols.T.astype(jnp.bfloat16), grad_cols.T.astype(jnp.bfloat16), gate_grad)


def solution(mesh):
    placed = (
        P("grp", ("side", "rep")),
        P("grp", ("side", "rep")),
        P("grp", None),
        P("grp", None),
        P("grp", None, ("side", "rep")),
        P("grp", None, ("side", "rep")),
        P("grp", ("side", "rep"), None),
    )
    return jax.shard_map(
        local,
        mesh=mesh,
        in_specs=placed,
        out_specs=(P("grp", ("side", "rep")), P("grp", ("side", "rep")), P("grp", None)),
        check_vma=False,
    )
```

profile of v0, /device:TPU:2, one launch (start us, length us, event | category | flops | bytes accessed | tf_op | source)
XLA Modules:
  0.0 446.8 jit_solution(11921651392973204754)
XLA Ops:
  7.2 0.9 copy.19
  8.4 0.2 reduce_window_sum.11
  8.6 0.2 select_reduce_fusion
  8.7 0.3 fusion.17
  9.0 0.9 fusion.8
  9.9 33.4 %all_to_all.30 = bf16[32,8,128]{2,1,0:T(8,128)(2,1)} all-to-all(bf16[32,8,128]{2,1,0:T(8,128)(2,1)S(1)} %fusion.8), channel_id=1, replica_groups=mesh['side'=2,'grp'=32,'rep'=16] {'grp'}, dimensions={0} | all-to-all | bytes 131072 | tf_op jit(solution)/shard_map/all_to_all | solution.py:50
  43.4 0.9 fusion.7
  44.3 17.7 %all_to_all.31 = bf16[32,8,128]{2,1,0:T(8,128)(2,1)} all-to-all(bf16[32,8,128]{2,1,0:T(8,128)(2,1)S(1)} %fusion.7), channel_id=1, replica_groups=mesh['side'=2,'grp'=32,'rep'=16] {'grp'}, dimensions={0} | all-to-all | bytes 131072 | tf_op jit(solution)/shard_map/all_to_all | solution.py:51
  62.1 0.8 copy.20
  62.9 0.1 reshape.114
  63.3 16.1 %all_to_all.32 = bf16[32,1,8]{2,1,0:T(2,128)(2,1)S(1)} all-to-all(bf16[32,1,8]{2,1,0:T(2,128)(2,1)S(1)} %all_to_all.24), channel_id=1, replica_groups=mesh['side'=2,'grp'=32,'rep'=16] {'grp'}, dimensions={0} | all-to-all | bytes 1024 | tf_op jit(solution)/shard_map/all_to_all | solution.py:52
  79.5 48.0 %all-gather.5.cloned.1.call-done = bf16[32,8,4096]{2,1,0:T(8,128)(2,1)} async-done(((bf16[32,8,128]{2,1,0:T(8,128)(2,1)}), bf16[32,8,4096]{2,1,0:T(8,128)(2,1)}) %all-gather.5.cloned.1.call-update) | async-done | bytes 2097168 | tf_op jit(solution)/shard_map/all_gather | solution.py:56
  127.5 2.7 fusion.1
  130.2 2.5 fusion.3
  132.8 89.0 %all-gather.3.cloned.1.call-done = bf16[32,8,4096]{2,1,0:T(8,128)(2,1)} async-done(((bf16[32,8,128]{2,1,0:T(8,128)(2,1)}), bf16[32,8,4096]{2,1,0:T(8,128)(2,1)}) %all-gather.3.cloned.1.call-update) | async-done | bytes 2097168 | tf_op jit(solution)/shard_map/all_gather | solution.py:57
  221.8 2.4 multiply_reduce_fusion
  224.3 0.8 fusion.9
  225.1 0.8 fusion
  225.8 0.7 convolution_bitcast_fusion
  226.6 3.8 pad_maximum_fusion
  230.4 131.9 %psum.7 = f32[1,1,32,8]{3,2,1,0:T(8,128)} all-reduce(f32[1,1,32,8]{3,2,1,0:T(8,128)S(1)} %reshape.111), channel_id=1, replica_groups=mesh['side'=2,'grp'=32,'rep'=16] {'side','rep'}, use_global_device_ids=true, to_apply=%region_4.5 | all-reduce | flops 256 | bytes 2048 | tf_op jit(solution)/shard_map/psum | solution.py:70
  362.3 14.5 %all-to-all-start.4 = ((f32[1,1,32,8]{3,1,0,2:T(1,128)}), f32[1,1,32,8]{3,1,0,2:T(1,128)S(1)}, u32[]{:S(2)}, u32[]{:S(2)}) async-start(f32[1,1,32,8]{3,1,0,2:T(1,128)} %bitcast.14), calls=%async_computation.5 | async-start | bytes 32768 | tf_op jit(solution)/shard_map/all_to_all | solution.py:90
  376.8 28.6 %reduce-scatter.2.cloned.1.call-done = f32[128,512]{0,1:T(8,128)} async-done(((f32[4096,512]{0,1:T(8,128)}), f32[128,512]{0,1:T(8,128)}) %reduce-scatter.2.cloned.1.call-update) | async-done | bytes 262160 | tf_op jit(solution)/shard_map/reduce_scatter | solution.py:80
  405.5 1.7 copy.22
  407.1 14.7 %all-to-all-start.3 = ((f32[128,2,32,8]{0,3,1,2:T(8,128)}), f32[128,2,32,8]{0,3,1,2:T(8,128)S(1)}, u32[]{:S(2)}, u32[]{:S(2)}) async-start(f32[128,2,32,8]{0,3,1,2:T(8,128)} %copy.22), calls=%async_computation.4 | async-start | bytes 524288 | tf_op jit(solution)/shard_map/all_to_all | solution.py:89
  422.1 0.3 fusion.18
  422.4 0.5 broadcast.79
  423.0 0.7 reduce.7
  423.7 0.8 fusion.19
  424.5 14.1 %all-to-all-done.3 = f32[128,2,32,8]{0,3,1,2:T(8,128)S(1)} async-done(((f32[128,2,32,8]{0,3,1,2:T(8,128)}), f32[128,2,32,8]{0,3,1,2:T(8,128)S(1)}, u32[]{:S(2)}, u32[]{:S(2)}) %all-to-all-start.3) | async-done | bytes 262176 | tf_op jit(solution)/shard_map/all_to_all | solution.py:89
  438.6 0.8 convolution_convert_fusion.2
  439.4 0.8 convolution_convert_fusion.3
  (28 shorter events, 1.3 us)
Async XLA Ops:
  7.2 214.7 %copy-start = (bf16[1,128,4096]{2,1,0:T(8,128)(2,1)S(1)}, bf16[1,128,4096]{2,1,0:T(8,128)(2,1)}, u32[]{:S(2)}) copy-start(bf16[1,128,4096]{2,1,0:T(8,128)(2,1)} %param.13) | copy-start | bytes 3145732
  7.2 123.0 %copy-start.1 = (bf16[1,4096,128]{2,1,0:T(8,128)(2,1)S(1)}, bf16[1,4096,128]{2,1,0:T(8,128)(2,1)}, u32[]{:S(2)}) copy-start(bf16[1,4096,128]{2,1,0:T(8,128)(2,1)} %param.12) | copy-start | bytes 3145732
  7.2 120.3 %all-gather.5.cloned.1.call-start = ((), (), s32[]{:S(2)}) async-start(), calls=%async_computation.7 | async-start | bytes 2162688 | tf_op jit(solution)/shard_map/all_gather | solution.py:56
  43.4 178.5 %all-gather.3.cloned.1.call-start = ((), (), s32[]{:S(2)}) async-start(), calls=%async_computation.6 | async-start | bytes 2162688 | tf_op jit(solution)/shard_map/all_gather | solution.py:57
  62.1 343.4 %reduce-scatter.2.cloned.1.call-start = ((), (), s32[]{:S(2)}) async-start(), calls=%async_computation.8 | async-start | bytes 8650752 | tf_op jit(solution)/shard_map/reduce_scatter | solution.py:80
  130.2 94.0 %copy-start.2 = (bf16[1,4096,128]{2,1,0:T(8,128)(2,1)S(1)}, bf16[1,4096,128]{2,1,0:T(8,128)(2,1)}, u32[]{:S(2)}) copy-start(bf16[1,4096,128]{2,1,0:T(8,128)(2,1)} %param.11) | copy-start | bytes 3145732
  362.3 44.8 %all-to-all-start.4 = ((f32[1,1,32,8]{3,1,0,2:T(1,128)}), f32[1,1,32,8]{3,1,0,2:T(1,128)S(1)}, u32[]{:S(2)}, u32[]{:S(2)}) async-start(f32[1,1,32,8]{3,1,0,2:T(1,128)} %bitcast.14), calls=%async_computation.5 | async-start | bytes 32768 | tf_op jit(solution)/shard_map/all_to_all | solution.py:90
  407.1 31.4 %all-to-all-start.3 = ((f32[128,2,32,8]{0,3,1,2:T(8,128)}), f32[128,2,32,8]{0,3,1,2:T(8,128)S(1)}, u32[]{:S(2)}, u32[]{:S(2)}) async-start(f32[128,2,32,8]{0,3,1,2:T(8,128)} %copy.22), calls=%async_computation.4 | async-start | bytes 524288 | tf_op jit(solution)/shard_map/all_to_all | solution.py:89
Sparse Core Ops, SparseCore 0:
  43.5 84.0 all-gather.4
  131.8 89.9 all-gather.2
  230.5 174.9 reduce-scatter.1
where the time goes:
time: 448 us; the launch traced here: 447 us
  blocking collectives  199 us (44%)
  waiting for transfers between devices  180 us (40%)
  starting transfers between devices  29.3 us (7%)
  matrix products  14.9 us (3%)
  between operations  13.9 us (3%)
  other arithmetic  5.04 us (1%)
  local copies, waits for them, and re-layouts  4.73 us (1%)
    psum x1, blocking collectives, local(): gate_total = lax.psum(partial_gate, ('side', 'rep'))  132 us
    all_gather x1, waiting for transfers between devices, local(): lax.all_gather(recv_dy, ('side', 'rep'), axis=2, tiled=True)  89 us
    all_gather x1, waiting for transfers between devices, local(): lax.all_gather(recv_x, ('side', 'rep'), axis=2, tiled=True)  48 us
    all_to_all x1, blocking collectives, local(): lax.all_to_all(send_x, 'grp', split_axis=0, concat_axis=0, tiled=True)  33.4 us
    reduce_scatter x1, waiting for transfers between devices, local(): lax.psum_scatter(jnp.concatenate([input_term, layer_term], axis=1), ('sid...  28.6 us
    all_to_all x1, blocking collectives, local(): lax.all_to_all(send_dy, 'grp', split_axis=0, concat_axis=0, tiled=True)  17.7 us
    all_to_all x1, blocking collectives, local(): lax.all_to_all(send_gate, 'grp', split_axis=0, concat_axis=0, tiled=True)  16.1 us
    all_to_all x1, starting transfers between devices, local(): lax.all_to_all(parts, 'grp', split_axis=2, concat_axis=2, tiled=True)  14.7 us
  transfers between devices with their start and end apart: 5, of which 4 were waited for; matrix products, arithmetic and copies ran while one was open for 3% of the time, Pallas kernels for 0%

commit v1 on v0

v1 whole, which is shorter than its diff:
```python
import functools

import jax
import jax.numpy as jnp
from jax import lax
from jax.experimental import pallas as pl
from jax.experimental.pallas import tpu as pltpu
from jax.sharding import PartitionSpec as P

CAP = 8
BF = jnp.bfloat16
F32 = jnp.float32
NT = (((1,), (1,)), ((), ()))
TN = (((0,), (0,)), ((), ()))
VM = pl.BlockSpec(memory_space=pltpu.VMEM)
SM = pl.BlockSpec(memory_space=pltpu.SMEM)


def slot_masks(route_ref, groups):
    rows = route_ref.shape[0]
    first, second = route_ref[:, 0:1], route_ref[:, 1:2]
    lanes = lax.broadcasted_iota(jnp.int32, (rows, 128), 1)
    hot0 = (lanes == first).astype(F32)
    hot1 = (lanes == second).astype(F32)
    below = (
        lax.broadcasted_iota(jnp.int32, (rows, rows), 1)
        < lax.broadcasted_iota(jnp.int32, (rows, rows), 0)
    ).astype(BF)
    earlier0 = jnp.dot(below, hot0.astype(BF), preferred_element_type=F32)
    earlier1 = jnp.dot(below, hot1.astype(BF), preferred_element_type=F32)
    count0 = jnp.sum(hot0, axis=0, keepdims=True)
    slot0 = jnp.sum(earlier0 * hot0, axis=1, keepdims=True).astype(jnp.int32)
    slot1 = jnp.sum((earlier1 + count0) * hot1, axis=1, keepdims=True).astype(jnp.int32)
    wide = lax.broadcasted_iota(jnp.int32, (rows, groups * CAP), 1)
    return (
        (wide == first * CAP + slot0).astype(F32),
        (wide == second * CAP + slot1).astype(F32),
    )


def dispatch_kernel(groups, tok_ref, dy_ref, route_ref, out_ref):
    mask0, mask1 = slot_masks(route_ref, groups)
    picks = (mask0 + mask1).astype(BF)
    for part, ref in enumerate((tok_ref, dy_ref)):
        rows = lax.dot_general(picks, ref[...], TN, preferred_element_type=F32)
        out_ref[:, part * CAP : (part + 1) * CAP, :] = rows.reshape(groups, CAP, -1).astype(BF)


def combine_kernel(groups, back_ref, route_ref, gate_ref, layer_ref, grad_ref, gg_ref):
    mask0, mask1 = slot_masks(route_ref, groups)
    weights = gate_ref[...].astype(F32)
    mix = (mask0 * weights[:, 0:1] + mask1 * weights[:, 1:2]).astype(BF)
    slots = groups * CAP
    back = back_ref[...].astype(F32)
    layer = back[:, 0:CAP].reshape(slots, -1).astype(BF)
    grad = back[:, CAP : 2 * CAP].reshape(slots, -1).astype(BF)
    sums = back[:, 2 * CAP :].reshape(slots, -1).astype(BF)
    layer_ref[...] = jnp.dot(mix, layer, preferred_element_type=F32).astype(BF)
    grad_ref[...] = jnp.dot(mix, grad, preferred_element_type=F32).astype(BF)
    gg0 = jnp.dot(mask0.astype(BF), sums, preferred_element_type=F32)
    gg1 = jnp.dot(mask1.astype(BF), sums, preferred_element_type=F32)
    gg_ref[...] = jnp.concatenate([gg0[:, 0:1], gg1[:, 0:1]], axis=1)


def weight_kernel(pos_ref, wg_ref, wu_ref, wd_ref, out_ref):
    other = 1 - pos_ref[1]
    sides, ys = wg_ref.shape[0], wg_ref.shape[1]
    for s in range(sides):
        for y in range(ys):
            out_ref[0, s, y] = wg_ref[s, y, other]
            out_ref[1, s, y] = wu_ref[s, y, other]
            start = pl.multiple_of(((s * ys + y) * 2 + other) * 128, 128)
            out_ref[2, s, y] = wd_ref[:, pl.ds(start, 128)]


def pre_kernel(pos_ref, x_ref, dyo_ref, dyp_ref, wg_ref, wu_ref, wd_ref, wr_ref, out_ref):
    side, core = pos_ref[0], pos_ref[1]
    ys = wg_ref.shape[1]
    f = wg_ref.shape[-1]
    gate = up = back = None
    for rel in range(2):
        sd = side if rel == 0 else 1 - side
        x = jnp.concatenate([x_ref[y, rel] for y in range(ys)], axis=1)
        dy_from = dyo_ref if rel == 0 else dyp_ref
        dy = jnp.concatenate([dy_from[y] for y in range(ys)], axis=1)
        wg = jnp.concatenate(
            [wg_ref[sd, :, core].reshape(ys * 128, f), wr_ref[0, sd].reshape(ys * 128, f)], axis=1
        )
        wu = jnp.concatenate(
            [wu_ref[sd, :, core].reshape(ys * 128, f), wr_ref[1, sd].reshape(ys * 128, f)], axis=1
        )
        own = [
            wd_ref[:, pl.ds(pl.multiple_of(((sd * ys + y) * 2 + core) * 128, 128), 128)]
            for y in range(ys)
        ]
        wd = jnp.concatenate(
            [
                jnp.concatenate(own, axis=1),
                jnp.concatenate([wr_ref[2, sd, y] for y in range(ys)], axis=1),
            ],
            axis=0,
        )
        g = jnp.dot(x, wg, preferred_element_type=F32)
        u = jnp.dot(x, wu, preferred_element_type=F32)
        b = lax.dot_general(dy, wd, NT, preferred_element_type=F32)
        gate, up, back = (g, u, b) if rel == 0 else (gate + g, up + u, back + b)
    for at, value in enumerate((gate, up, back)):
        out_ref[:, at * f : (at + 1) * f] = value[:, :f]
        out_ref[:, (3 + at) * f : (4 + at) * f] = value[:, f:]


def post_kernel(
    pos_ref, mine_ref, theirs_ref, wg_ref, wu_ref, wd_ref, wr_ref, g_ref, keep_ref, send_ref
):
    side, core = pos_ref[0], pos_ref[1]
    ys = wg_ref.shape[1]
    f = wg_ref.shape[-1]
    rows = mine_ref.shape[0]

    def total(at):
        own = mine_ref[:, at * f : (at + 1) * f] + theirs_ref[:, (3 + at) * f : (4 + at) * f]
        par = mine_ref[:, (3 + at) * f : (4 + at) * f] + theirs_ref[:, at * f : (at + 1) * f]
        return jnp.concatenate([own, par], axis=1)

    gate, up, back = total(0), total(1), total(2)
    sigma = jax.nn.sigmoid(gate)
    active = gate * sigma
    hidden = (active * up).astype(BF)
    ones = jnp.ones((8, 2 * f), F32)
    sums = lax.dot_general(
        ones,
        hidden.astype(F32) * back,
        NT,
        preferred_element_type=F32,
        precision=lax.Precision.HIGHEST,
    )
    top = lax.broadcasted_iota(jnp.int32, (8, rows // 2), 0) == 0
    packed = jnp.where(top, sums[:, : rows // 2], sums[:, rows // 2 :]).astype(BF)
    d_gate = (back * up * sigma * (1.0 + gate * (1.0 - sigma))).astype(BF)
    d_up = (back * active).astype(BF)
    both = jnp.concatenate([d_gate, d_up], axis=1)
    for rel in range(2):
        sd = side if rel == 0 else 1 - side
        for y in range(ys):
            start = pl.multiple_of(((sd * ys + y) * 2 + core) * 128, 128)
            wd = jnp.concatenate([wd_ref[:, pl.ds(start, 128)], wr_ref[2, sd, y]], axis=0)
            wgu = jnp.concatenate(
                [wg_ref[sd, y, core], wr_ref[0, sd, y], wu_ref[sd, y, core], wr_ref[1, sd, y]],
                axis=1,
            )
            layer = jnp.dot(hidden, wd, preferred_element_type=F32).astype(BF)
            if rel == 0:
                keep_ref[y] = layer
            else:
                send_ref[y] = layer
            grad = lax.dot_general(both, wgu, NT, preferred_element_type=F32)
            g_ref[y, rel * rows : (rel + 1) * rows, :] = grad.astype(BF)
    for y in range(ys):
        g_ref[y, 2 * rows :, :] = packed


def add_kernel(a_ref, b_ref, o_ref):
    o_ref[...] = (a_ref[...].astype(F32) + b_ref[...].astype(F32)).astype(BF)


def half_kernel(g_ref, keep_ref, send_ref):
    rows = keep_ref.shape[0] - 8
    acc = g_ref[0].astype(F32)
    for y in range(1, g_ref.shape[0]):
        acc = acc + g_ref[y].astype(F32)
    keep_ref[:rows] = acc[:rows]
    keep_ref[rows:] = acc[2 * rows :]
    send_ref[:rows] = acc[rows : 2 * rows].astype(BF)
    send_ref[rows:] = acc[2 * rows :].astype(BF)


def return_kernel(groups, layer_ref, keep_ref, recv_ref, out_ref):
    rows = groups * CAP
    layer = layer_ref[0].astype(F32)
    for y in range(1, layer_ref.shape[0]):
        layer = layer + layer_ref[y].astype(F32)
    both = keep_ref[...] + recv_ref[...].astype(F32)
    out_ref[:, :CAP] = layer.reshape(groups, CAP, -1).astype(BF)
    out_ref[:, CAP : 2 * CAP] = both[:rows].reshape(groups, CAP, -1).astype(BF)
    half = rows // 2
    eye = lax.broadcasted_iota(jnp.int32, (half, half), 0) == lax.broadcasted_iota(
        jnp.int32, (half, half), 1
    )
    for part in range(2):
        line = jnp.broadcast_to(both[rows + part : rows + part + 1, :], (half, half))
        column = jnp.sum(jnp.where(eye, line, 0.0), axis=1, keepdims=True)
        wide = jnp.broadcast_to(column, (half, half)).reshape(groups // 2, CAP, half)
        out_ref[part * groups // 2 : (part + 1) * groups // 2, 2 * CAP :] = wide.astype(BF)


def call(body, outs, ins, flops=0):
    shapes = [jax.ShapeDtypeStruct(s, d) for s, d in outs]
    size = sum(a.size * a.dtype.itemsize for a in ins)
    size += sum(s.size * s.dtype.itemsize for s in shapes)
    specs = [SM if a.dtype == jnp.int32 and a.ndim == 1 else VM for a in ins]
    one = len(shapes) == 1
    return pl.pallas_call(
        body,
        out_shape=shapes[0] if one else shapes,
        in_specs=specs,
        out_specs=VM if one else [VM] * len(shapes),
        compiler_params=pltpu.CompilerParams(vmem_limit_bytes=40 << 20),
        cost_estimate=pl.CostEstimate(flops=flops, bytes_accessed=size, transcendentals=0),
    )(*ins)


def local(tokens, grad_out, route, gate, w_gate, w_up, w_down):
    groups = lax.axis_size("grp")
    ys = lax.axis_size("rep") // 2
    width = tokens.shape[1]
    rows = groups * CAP
    f = w_gate.shape[2]
    rep = lax.axis_index("rep")
    pos = jnp.stack([lax.axis_index("side"), rep % 2]).astype(jnp.int32)
    columns = [[2 * y + c for y in range(ys)] for c in range(2)]
    swap_core = [(i, i ^ 1) for i in range(2 * ys)]
    swap_side = [(0, 1), (1, 0)]

    def over_y(a):
        return lax.all_to_all(a, "rep", 0, 0, tiled=True, axis_index_groups=columns)

    wg = w_gate.reshape(2, ys, 2, width, f)
    wu = w_up.reshape(2, ys, 2, width, f)
    wd = w_down.reshape(f, -1)

    send = call(
        functools.partial(dispatch_kernel, groups),
        [((groups, 2 * CAP, width), BF)],
        [tokens, grad_out, route],
    )
    w_send = call(weight_kernel, [((3, 2, ys, width, f), BF)], [pos, wg, wu, wd])
    w_recv = lax.ppermute(w_send, "rep", swap_core)
    recv = lax.all_to_all(send, "grp", 0, 0, tiled=True)
    x = recv[:, :CAP].reshape(rows, width)
    dy = recv[:, CAP:].reshape(rows, width)

    x_other = lax.ppermute(x, "side", swap_side)
    dy_own = over_y(jnp.broadcast_to(dy[None], (ys, rows, width)))
    dy_other = lax.ppermute(dy_own, "side", swap_side)
    x_pair = jnp.stack([x, x_other])
    x_all = over_y(jnp.broadcast_to(x_pair[None], (ys, 2, rows, width)))

    depth = ys * 2 * width
    mine = call(
        pre_kernel,
        [((rows, 6 * f), F32)],
        [pos, x_all, dy_own, dy_other, wg, wu, wd, w_recv],
        flops=2 * rows * depth * 2 * f * 3,
    )
    theirs = lax.ppermute(mine, "rep", swap_core)
    grads, keep, away = call(
        post_kernel,
        [((ys, 2 * rows + 8, width), BF), ((ys, rows, width), BF), ((ys, rows, width), BF)],
        [pos, mine, theirs, wg, wu, wd, w_recv],
        flops=2 * rows * depth * 2 * f * 3,
    )
    arrived = lax.ppermute(away, "side", swap_side)
    grads = over_y(grads)
    g_keep, g_send = call(
        half_kernel, [((rows + 8, width), F32), ((rows + 8, width), BF)], [grads]
    )
    g_recv = lax.ppermute(g_send, "side", swap_side)
    layer = over_y(call(add_kernel, [((ys, rows, width), BF)], [keep, arrived]))
    out = call(
        functools.partial(return_kernel, groups),
        [((groups, 3 * CAP, width), BF)],
        [layer, g_keep, g_recv],
    )
    home = lax.all_to_all(out, "grp", 0, 0, tiled=True)
    layer_out, grad_tokens, gate_grad = call(
        functools.partial(combine_kernel, groups),
        [(tokens.shape, BF), (tokens.shape, BF), (route.shape, F32)],
        [home, route, gate],
    )
    return layer_out, grad_tokens, gate_grad


def solution(mesh):
    placed = (
        P("grp", ("side", "rep")),
        P("grp", ("side", "rep")),
        P("grp", None),
        P("grp", None),
        P("grp", None, ("side", "rep")),
        P("grp", None, ("side", "rep")),
        P("grp", ("side", "rep"), None),
    )
    return jax.shard_map(
        local,
        mesh=mesh,
        in_specs=placed,
        out_specs=(P("grp", ("side", "rep")), P("grp", ("side", "rep")), P("grp", None)),
        check_vma=False,
    )
```

time: 448 us -> 195 us (0.44)
  the two profiles are of different devices: /device:TPU:2 before, /device:TPU:4 now
where the time goes in v1:
time: 195 us; the launch traced here: 194 us
  waiting for transfers between devices  93.3 us (48%)
  starting transfers between devices  41.9 us (21%)
  blocking collectives  36.4 us (19%)
  local copies, waits for them, and re-layouts  12 us (6%)
  Pallas kernels  9.45 us (5%)
    all_to_all x4, waiting for transfers between devices, over_y(): return lax.all_to_all(a, 'rep', 0, 0, tiled=True, axis_index_groups=columns)  37.7 us
    all_to_all x1, blocking collectives, local(): recv = lax.all_to_all(send, 'grp', 0, 0, tiled=True)  36.4 us
    all_to_all x1, waiting for transfers between devices, local(): home = lax.all_to_all(out, 'grp', 0, 0, tiled=True)  19.7 us
    all_to_all x4, starting transfers between devices, over_y(): return lax.all_to_all(a, 'rep', 0, 0, tiled=True, axis_index_groups=columns)  18.5 us
    ppermute x1, waiting for transfers between devices, local(): arrived = lax.ppermute(away, 'side', swap_side)  14.6 us
    ppermute x1, waiting for transfers between devices, local(): dy_other = lax.ppermute(dy_own, 'side', swap_side)  13.4 us
    pallas_call x8, Pallas kernels, call(): pl.pallas_call(body, out_shape=shapes[0] if one else shapes, in_specs=spe...  9.45 us
    unnamed x34, local copies, waits for them, and re-layouts  9.34 us
  transfers between devices with their start and end apart: 11, of which 10 were waited for; matrix products, arithmetic and copies ran while one was open for 0% of the time, Pallas kernels for 1%

profile of v1, /device:TPU:4, one launch (start us, length us, event | category | flops | bytes accessed | tf_op | source)
XLA Modules:
  0.0 194.0 jit_solution(12974270236019256479)
XLA Ops:
  3.4 36.4 %all_to_all.30 = bf16[32,16,128]{2,1,0:T(8,128)(2,1)S(1)} all-to-all(bf16[32,16,128]{2,1,0:T(8,128)(2,1)S(1)} %shard_map.94), channel_id=1, replica_groups=mesh['side'=2,'grp'=32,'rep'=16] {'grp'}, dimensions={0} | all-to-all | bytes 262144 | tf_op jit(solution)/shard_map/all_to_all | solution.py:238
  39.9 0.9 broadcast_in_dim.15
  40.7 7.1 %all-to-all-start.2 = ((bf16[8,256,128]{2,1,0:T(8,128)(2,1)}), bf16[8,256,128]{2,1,0:T(8,128)(2,1)}, u32[]{:S(2)}, u32[]{:S(2)}) async-start(bf16[8,256,128]{2,1,0:T(8,128)(2,1)} %broadcast_in_dim.15), calls=%async_computation.2 | async-start | bytes 1048576 | tf_op jit(solution)/shard_map/all_to_all | solution.py:225
  47.8 2.7 %collective-permute-start = (bf16[256,128]{1,0:T(8,128)(2,1)S(1)}, bf16[256,128]{1,0:T(8,128)(2,1)S(1)}, u32[]{:S(2)}, u32[]{:S(2)}) collective-permute-start(bf16[256,128]{1,0:T(8,128)(2,1)S(1)} %get-tuple-element.17), channel_id=1, source_target_pairs={{0,512},{512,0},{1,513},{513,1},{2,514},{514,2},{3,515},{515,3},{4... | collective-permute-start | bytes 196616 | tf_op jit(solution)/shard_map/ppermute | solution.py:242
  50.5 4.9 %collective-permute-done = bf16[256,128]{1,0:T(8,128)(2,1)S(1)} collective-permute-done((bf16[256,128]{1,0:T(8,128)(2,1)S(1)}, bf16[256,128]{1,0:T(8,128)(2,1)S(1)}, u32[]{:S(2)}, u32[]{:S(2)}) %collective-permute-start) | collective-permute-done | bytes 65568 | tf_op jit(solution)/shard_map/ppermute | solution.py:242
  55.5 7.4 %all-to-all-done.2.dyo_ref = bf16[8,256,128]{2,1,0:T(8,128)(2,1)} async-done(((bf16[8,256,128]{2,1,0:T(8,128)(2,1)}), bf16[8,256,128]{2,1,0:T(8,128)(2,1)}, u32[]{:S(2)}, u32[]{:S(2)}) %all-to-all-start.2) | async-done | bytes 524320 | tf_op jit(solution)/shard_map/all_to_all | solution.py:225
  62.9 1.2 broadcast_in_dim.6
  64.1 4.2 %all-to-all-start.1 = ((bf16[8,2,256,128]{3,2,1,0:T(8,128)(2,1)}), bf16[8,2,256,128]{3,2,1,0:T(8,128)(2,1)}, u32[]{:S(2)}, u32[]{:S(2)}) async-start(bf16[8,2,256,128]{3,2,1,0:T(8,128)(2,1)} %broadcast_in_dim.6), calls=%async_computation.1 | async-start | bytes 2097152 | tf_op jit(solution)/shard_map/all_to_all | solution.py:225
  69.2 1.9 collective-permute-start.2
  71.1 2.7 %collective-permute-start.1 = (bf16[8,256,128]{2,1,0:T(8,128)(2,1)}, bf16[8,256,128]{2,1,0:T(8,128)(2,1)S(1)}, u32[]{:S(2)}, u32[]{:S(2)}) collective-permute-start(bf16[8,256,128]{2,1,0:T(8,128)(2,1)} %all-to-all-done.2.dyo_ref), channel_id=1, source_target_pairs={{0,512},{512,0},{1,513},{513,1},{2,514},{514,2},{3,515},{515,3},{4... | collective-permute-start | bytes 1572872 | tf_op jit(solution)/shard_map/ppermute | solution.py:244
  74.5 1.2 copy-done.3
  75.7 13.4 %collective-permute-done.1.dyp_ref = bf16[8,256,128]{2,1,0:T(8,128)(2,1)S(1)} collective-permute-done((bf16[8,256,128]{2,1,0:T(8,128)(2,1)}, bf16[8,256,128]{2,1,0:T(8,128)(2,1)S(1)}, u32[]{:S(2)}, u32[]{:S(2)}) %collective-permute-start.1) | collective-permute-done | bytes 524320 | tf_op jit(solution)/shard_map/ppermute | solution.py:244
  89.9 3.9 %all-to-all-done.1.x_ref = bf16[8,2,256,128]{3,2,1,0:T(8,128)(2,1)} async-done(((bf16[8,2,256,128]{3,2,1,0:T(8,128)(2,1)}), bf16[8,2,256,128]{3,2,1,0:T(8,128)(2,1)}, u32[]{:S(2)}, u32[]{:S(2)}) %all-to-all-start.1) | async-done | bytes 1048608 | tf_op jit(solution)/shard_map/all_to_all | solution.py:225
  93.8 1.4 copy-done.4
  95.2 1.0 copy-done.10
  96.2 2.5 %shard_map.96.mine_ref = f32[256,768]{1,0:T(8,128)S(1)} custom-call(s32[2]{0:T(128)S(1)} %pad_add_fusion.pos_ref, bf16[8,2,256,128]{3,2,1,0:T(8,128)(2,1)} %all-to-all-done.1.x_ref, bf16[8,256,128]{2,1,0:T(8,128)(2,1)} %all-to-all-done.2.dyo_ref, bf16[8,256,128]{2,1,0:T(8,128)(2,1)S(1)} %copy-done.10, bf16[2,8,2,128,128]{4,3,2,1,0:T(8,128)(2,1)S(1)} %bitcast.13, ...), custom_call_target="tpu_custom_call" | custom-call | flops 805306368 | bytes 7602184 | tf_op jit(solution)/shard_map/pallas_call | solution.py:202
  98.7 1.9 collective-permute-start.3
  100.7 2.3 %collective-permute-done.3.theirs_ref = f32[256,768]{1,0:T(8,128)S(1)} collective-permute-done((f32[256,768]{1,0:T(8,128)S(1)}, f32[256,768]{1,0:T(8,128)S(1)}, u32[]{:S(2)}, u32[]{:S(2)}) %collective-permute-start.3) | collective-permute-done | bytes 786464 | tf_op jit(solution)/shard_map/ppermute | solution.py:255
  102.9 2.7 %shard_map.97 = (bf16[8,520,128]{2,1,0:T(8,128)(2,1)S(1)}, bf16[8,256,128]{2,1,0:T(8,128)(2,1)S(1)}, bf16[8,256,128]{2,1,0:T(8,128)(2,1)S(1)}) custom-call(s32[2]{0:T(128)S(1)} %pad_add_fusion.pos_ref, f32[256,768]{1,0:T(8,128)S(1)} %shard_map.96.mine_ref, f32[256,768]{1,0:T(8,128)S(1)} %collective-permute-done.3.theirs_ref, ...), custom_call_target="tpu_custom_call" | custom-call | flops 805306368 | bytes 8405000 | tf_op jit(solution)/shard_map/pallas_call | solution.py:202
  105.6 1.0 copy-done.6
  108.1 3.7 %all-to-all-start.4 = ((bf16[8,520,128]{2,1,0:T(8,128)(2,1)}), bf16[8,520,128]{2,1,0:T(8,128)(2,1)S(1)}, u32[]{:S(2)}, u32[]{:S(2)}) async-start(bf16[8,520,128]{2,1,0:T(8,128)(2,1)} %copy-done.6), calls=%async_computation.4 | async-start | bytes 2129920 | tf_op jit(solution)/shard_map/all_to_all | solution.py:225
  111.9 2.7 %collective-permute-start.4 = (bf16[8,256,128]{2,1,0:T(8,128)(2,1)S(1)}, bf16[8,256,128]{2,1,0:T(8,128)(2,1)S(1)}, u32[]{:S(2)}, u32[]{:S(2)}) collective-permute-start(bf16[8,256,128]{2,1,0:T(8,128)(2,1)S(1)} %copy-done.14), channel_id=1, source_target_pairs={{0,512},{512,0},{1,513},{513,1},{2,514},{514,2},{3,515},{515,3},{4... | collective-permute-start | bytes 1572872 | tf_op jit(solution)/shard_map/ppermute | solution.py:262
  114.6 14.6 %collective-permute-done.4.b_ref = bf16[8,256,128]{2,1,0:T(8,128)(2,1)S(1)} collective-permute-done((bf16[8,256,128]{2,1,0:T(8,128)(2,1)S(1)}, bf16[8,256,128]{2,1,0:T(8,128)(2,1)S(1)}, u32[]{:S(2)}, u32[]{:S(2)}) %collective-permute-start.4) | collective-permute-done | bytes 524320 | tf_op jit(solution)/shard_map/ppermute | solution.py:262
  129.2 0.9 shard_map.98
  130.1 11.4 %all-to-all-done.4.g_ref = bf16[8,520,128]{2,1,0:T(8,128)(2,1)S(1)} async-done(((bf16[8,520,128]{2,1,0:T(8,128)(2,1)}), bf16[8,520,128]{2,1,0:T(8,128)(2,1)S(1)}, u32[]{:S(2)}, u32[]{:S(2)}) %all-to-all-start.4) | async-done | bytes 1064992 | tf_op jit(solution)/shard_map/all_to_all | solution.py:225
  141.5 3.5 %all-to-all-start.3 = ((bf16[8,256,128]{2,1,0:T(8,128)(2,1)}), bf16[8,256,128]{2,1,0:T(8,128)(2,1)S(1)}, u32[]{:S(2)}, u32[]{:S(2)}) async-start(bf16[8,256,128]{2,1,0:T(8,128)(2,1)} %shard_map.98), calls=%async_computation.3 | async-start | bytes 1048576 | tf_op jit(solution)/shard_map/all_to_all | solution.py:225
  145.2 2.7 %collective-permute-start.5 = (bf16[264,128]{1,0:T(8,128)(2,1)S(1)}, bf16[264,128]{1,0:T(8,128)(2,1)S(1)}, u32[]{:S(2)}, u32[]{:S(2)}) collective-permute-start(bf16[264,128]{1,0:T(8,128)(2,1)S(1)} %get-tuple-element.12), channel_id=1, source_target_pairs={{0,512},{512,0},{1,513},{513,1},{2,514},{514,2},{3,515},{515,3},{4... | collective-permute-start | bytes 202760 | tf_op jit(solution)/shard_map/ppermute | solution.py:267
  147.9 15.0 %all-to-all-done.3.layer_ref = bf16[8,256,128]{2,1,0:T(8,128)(2,1)S(1)} async-done(((bf16[8,256,128]{2,1,0:T(8,128)(2,1)}), bf16[8,256,128]{2,1,0:T(8,128)(2,1)S(1)}, u32[]{:S(2)}, u32[]{:S(2)}) %all-to-all-start.3) | async-done | bytes 524320 | tf_op jit(solution)/shard_map/all_to_all | solution.py:225
  162.9 0.8 shard_map.100
  163.7 8.7 %all-to-all-start.5 = ((bf16[32,24,128]{2,1,0:T(8,128)(2,1)}), bf16[32,24,128]{2,1,0:T(8,128)(2,1)S(1)}, u32[]{:S(2)}, u32[]{:S(2)}) async-start(bf16[32,24,128]{2,1,0:T(8,128)(2,1)} %shard_map.100), calls=%async_computation.5 | async-start | bytes 393216 | tf_op jit(solution)/shard_map/all_to_all | solution.py:274
  172.5 19.7 %all-to-all-done.5.back_ref = bf16[32,24,128]{2,1,0:T(8,128)(2,1)S(1)} async-done(((bf16[32,24,128]{2,1,0:T(8,128)(2,1)}), bf16[32,24,128]{2,1,0:T(8,128)(2,1)S(1)}, u32[]{:S(2)}, u32[]{:S(2)}) %all-to-all-start.5) | async-done | bytes 196640 | tf_op jit(solution)/shard_map/all_to_all | solution.py:274
  192.2 1.1 shard_map.101
  (39 shorter events, 7.6 us)
Async XLA Ops:
  1.4 0.7 copy-start.11
  2.1 0.7 copy-start.12
  40.7 22.2 %all-to-all-start.2 = ((bf16[8,256,128]{2,1,0:T(8,128)(2,1)}), bf16[8,256,128]{2,1,0:T(8,128)(2,1)}, u32[]{:S(2)}, u32[]{:S(2)}) async-start(bf16[8,256,128]{2,1,0:T(8,128)(2,1)} %broadcast_in_dim.15), calls=%async_computation.2 | async-start | bytes 1048576 | tf_op jit(solution)/shard_map/all_to_all | solution.py:225
  47.8 7.7 %collective-permute-start = (bf16[256,128]{1,0:T(8,128)(2,1)S(1)}, bf16[256,128]{1,0:T(8,128)(2,1)S(1)}, u32[]{:S(2)}, u32[]{:S(2)}) collective-permute-start(bf16[256,128]{1,0:T(8,128)(2,1)S(1)} %get-tuple-element.17), channel_id=1, source_target_pairs={{0,512},{512,0},{1,513},{513,1},{2,514},{514,2},{3,515},{515,3},{4... | collective-permute-start | bytes 196616 | tf_op jit(solution)/shard_map/ppermute | solution.py:242
  55.5 12.9 %copy-start = (bf16[1,4096,128]{2,1,0:T(8,128)(2,1)S(1)}, bf16[1,4096,128]{2,1,0:T(8,128)(2,1)}, u32[]{:S(2)}) copy-start(bf16[1,4096,128]{2,1,0:T(8,128)(2,1)} %param.11) | copy-start | bytes 3145732
  55.5 12.9 %copy-start.1 = (bf16[1,4096,128]{2,1,0:T(8,128)(2,1)S(1)}, bf16[1,4096,128]{2,1,0:T(8,128)(2,1)}, u32[]{:S(2)}) copy-start(bf16[1,4096,128]{2,1,0:T(8,128)(2,1)} %param.12) | copy-start | bytes 3145732
  55.5 12.9 %copy-start.2 = (bf16[1,128,4096]{2,1,0:T(8,128)(2,1)S(1)}, bf16[1,128,4096]{2,1,0:T(8,128)(2,1)}, u32[]{:S(2)}) copy-start(bf16[1,128,4096]{2,1,0:T(8,128)(2,1)} %param.13) | copy-start | bytes 3145732
  64.1 29.7 %all-to-all-start.1 = ((bf16[8,2,256,128]{3,2,1,0:T(8,128)(2,1)}), bf16[8,2,256,128]{3,2,1,0:T(8,128)(2,1)}, u32[]{:S(2)}, u32[]{:S(2)}) async-start(bf16[8,2,256,128]{3,2,1,0:T(8,128)(2,1)} %broadcast_in_dim.6), calls=%async_computation.1 | async-start | bytes 2097152 | tf_op jit(solution)/shard_map/all_to_all | solution.py:225
  69.2 5.3 %collective-permute-start.2 = (bf16[3,2,8,128,128]{4,3,2,1,0:T(8,128)(2,1)S(1)}, bf16[3,2,8,128,128]{4,3,2,1,0:T(8,128)(2,1)S(1)}, u32[]{:S(2)}, u32[]{:S(2)}) collective-permute-start(bf16[3,2,8,128,128]{4,3,2,1,0:T(8,128)(2,1)S(1)} %shard_map.95), channel_id=1, source_target_pairs={{0,1},{1,0},{2,3},{3,2},{4,5},{5,4},{6,7},{7,6},{8,9},{9,8},{10,11... | collective-permute-start | bytes 4718600 | tf_op jit(solution)/shard_map/ppermute | solution.py:237
  71.1 17.9 %collective-permute-start.1 = (bf16[8,256,128]{2,1,0:T(8,128)(2,1)}, bf16[8,256,128]{2,1,0:T(8,128)(2,1)S(1)}, u32[]{:S(2)}, u32[]{:S(2)}) collective-permute-start(bf16[8,256,128]{2,1,0:T(8,128)(2,1)} %all-to-all-done.2.dyo_ref), channel_id=1, source_target_pairs={{0,512},{512,0},{1,513},{513,1},{2,514},{514,2},{3,515},{515,3},{4... | collective-permute-start | bytes 1572872 | tf_op jit(solution)/shard_map/ppermute | solution.py:244
  74.5 1.2 copy-start.3
  89.0 0.8 copy-start.9
  93.8 1.4 copy-start.4
  95.2 1.0 copy-start.10
  96.2 6.7 %copy-start.5 = (bf16[3,2,8,128,128]{4,3,2,1,0:T(8,128)(2,1)S(1)}, bf16[3,2,8,128,128]{4,3,2,1,0:T(8,128)(2,1)}, u32[]{:S(2)}) copy-start(bf16[3,2,8,128,128]{4,3,2,1,0:T(8,128)(2,1)} %copy-done.3) | copy-start | bytes 4718596
  98.7 4.2 %collective-permute-start.3 = (f32[256,768]{1,0:T(8,128)S(1)}, f32[256,768]{1,0:T(8,128)S(1)}, u32[]{:S(2)}, u32[]{:S(2)}) collective-permute-start(f32[256,768]{1,0:T(8,128)S(1)} %shard_map.96.mine_ref), channel_id=1, source_target_pairs={{0,1},{1,0},{2,3},{3,2},{4,5},{5,4},{6,7},{7,6},{8,9},{9,8},{10,11... | collective-permute-start | bytes 2359304 | tf_op jit(solution)/shard_map/ppermute | solution.py:255
  105.6 1.0 copy-start.6
  106.6 0.8 copy-start.7
  107.4 0.8 copy-start.13
  108.1 3.7 %copy-start.14 = (bf16[8,256,128]{2,1,0:T(8,128)(2,1)S(1)}, bf16[8,256,128]{2,1,0:T(8,128)(2,1)}, u32[]{:S(2)}) copy-start(bf16[8,256,128]{2,1,0:T(8,128)(2,1)} %copy-done.13) | copy-start | bytes 1572868
  108.1 21.1 %copy-start.8 = (bf16[8,256,128]{2,1,0:T(8,128)(2,1)S(1)}, bf16[8,256,128]{2,1,0:T(8,128)(2,1)}, u32[]{:S(2)}) copy-start(bf16[8,256,128]{2,1,0:T(8,128)(2,1)} %copy-done.7) | copy-start | bytes 1572868
  108.1 33.4 %all-to-all-start.4 = ((bf16[8,520,128]{2,1,0:T(8,128)(2,1)}), bf16[8,520,128]{2,1,0:T(8,128)(2,1)S(1)}, u32[]{:S(2)}, u32[]{:S(2)}) async-start(bf16[8,520,128]{2,1,0:T(8,128)(2,1)} %copy-done.6), calls=%async_computation.4 | async-start | bytes 2129920 | tf_op jit(solution)/shard_map/all_to_all | solution.py:225
  111.9 17.4 %collective-permute-start.4 = (bf16[8,256,128]{2,1,0:T(8,128)(2,1)S(1)}, bf16[8,256,128]{2,1,0:T(8,128)(2,1)S(1)}, u32[]{:S(2)}, u32[]{:S(2)}) collective-permute-start(bf16[8,256,128]{2,1,0:T(8,128)(2,1)S(1)} %copy-done.14), channel_id=1, source_target_pairs={{0,512},{512,0},{1,513},{513,1},{2,514},{514,2},{3,515},{515,3},{4... | collective-permute-start | bytes 1572872 | tf_op jit(solution)/shard_map/ppermute | solution.py:262
  130.1 42.3 %copy-start.15 = (bf16[64,2]{0,1:T(2,128)(2,1)S(1)}, bf16[64,2]{0,1:T(2,128)(2,1)}, u32[]{:S(2)}) copy-start(bf16[64,2]{0,1:T(2,128)(2,1)} %param.10) | copy-start | bytes 772
  141.5 21.4 %all-to-all-start.3 = ((bf16[8,256,128]{2,1,0:T(8,128)(2,1)}), bf16[8,256,128]{2,1,0:T(8,128)(2,1)S(1)}, u32[]{:S(2)}, u32[]{:S(2)}) async-start(bf16[8,256,128]{2,1,0:T(8,128)(2,1)} %shard_map.98), calls=%async_computation.3 | async-start | bytes 1048576 | tf_op jit(solution)/shard_map/all_to_all | solution.py:225
  145.2 17.7 %collective-permute-start.5 = (bf16[264,128]{1,0:T(8,128)(2,1)S(1)}, bf16[264,128]{1,0:T(8,128)(2,1)S(1)}, u32[]{:S(2)}, u32[]{:S(2)}) collective-permute-start(bf16[264,128]{1,0:T(8,128)(2,1)S(1)} %get-tuple-element.12), channel_id=1, source_target_pairs={{0,512},{512,0},{1,513},{513,1},{2,514},{514,2},{3,515},{515,3},{4... | collective-permute-start | bytes 202760 | tf_op jit(solution)/shard_map/ppermute | solution.py:267
  163.7 28.5 %all-to-all-start.5 = ((bf16[32,24,128]{2,1,0:T(8,128)(2,1)}), bf16[32,24,128]{2,1,0:T(8,128)(2,1)S(1)}, u32[]{:S(2)}, u32[]{:S(2)}) async-start(bf16[32,24,128]{2,1,0:T(8,128)(2,1)} %shard_map.100), calls=%async_computation.5 | async-start | bytes 393216 | tf_op jit(solution)/shard_map/all_to_all | solution.py:274
